TPU v7x, 32 devices: a whole 2x2x4 slice. The times are simulated.
32 devices in a mesh: groups: 2 (over y), genome: 4 (over z), ancestry: 2 (over x), trait: 2 (over core).
Axes of the slice: x: 2, y: 2, z: 4, core: 2. Of those that a mesh axis runs over, the one named last changes fastest.
Arguments:
- zscores: float32 [2, 64, 8192], P('ancestry', 'trait', ('groups', 'genome')), parts along dimension 2
- ld_diag: bfloat16 [2, 8192, 1024], P('ancestry', ('groups', 'genome')), parts along dimension 1, as said below
- ld_next: bfloat16 [2, 8192, 1024], P('ancestry', ('groups', 'genome')), parts along dimension 1
- prior_precision: float32 [2, 2], replicated, as said below
- chrom_cut: int32 [8], P('groups'), parts along dimension 0, may hold values from 0 to 2047
- band_width: int32 [8], P('groups'), parts along dimension 0, may hold values from 512 to 2047
Outputs:
- effect_sizes: float32 [2, 64, 8192], P('ancestry', 'trait', ('groups', 'genome')), parts along dimension 2
There are 2 independent parts, one for each index of `groups`. A program takes and returns all parts, laid end to end along the dimension named above; an argument that names none is the same for every part. Nothing has to cross between parts.
Inputs may be any that keep to these rules, and one draw needn't show every extreme that they name: `chrom_cut`: an entry below 1024 is the offset within its block of the first variant of a new chromosome; 1024 or more means the block holds no chromosome start. `band_width`: LD between two variants counts only when their distance is below the smaller width of their two blocks. `ld_diag`: each 1024 x 1024 diagonal block is symmetric with a positive diagonal. `prior_precision`: symmetric; each diagonal entry exceeds the sum of the magnitudes of the other entries of its row.
All inputs are finite; a program needn't handle non-finite values.
Results may differ from a plain program's by a relative error of at most 0.0025.
Values may be sent and summed in bfloat16 or wider, within the bound.
A program may use at most 64 MiB of HBM per device.

v0:
```python
import jax
import jax.numpy as jnp
from jax import lax
from jax.sharding import PartitionSpec as P

ITERS = 3


def passed_along(value, axis, steps):
    count = lax.axis_size(axis)
    leading, last = (max(0, -steps), min(count, count - steps))
    return lax.ppermute(value, axis, [(source, source + steps) for source in range(leading, last)])


def block_masks(block_len, cut_here, cut_after, width_here, width_after):
    row_ids = jnp.arange(block_len, dtype=jnp.int32)[:, None]
    col_ids = jnp.arange(block_len, dtype=jnp.int32)[None, :]
    opened = cut_here < block_len
    same_chrom = opened & (row_ids >= cut_here) == opened & (col_ids >= cut_here)
    inside = (jnp.abs(row_ids - col_ids) < width_here) & same_chrom
    before_cut = opened & (row_ids < cut_here)
    across = (
        (block_len + col_ids - row_ids < jnp.minimum(width_here, width_after))
        & jnp.logical_not(before_cut)
        & (col_ids < cut_after)
    )
    return (inside, across)


def curvature_sum(direction, image_vec):
    return lax.psum(jnp.sum(direction * image_vec, axis=1), ("genome", "ancestry"))


def residual_norm(residual, precond):
    return lax.psum(jnp.sum(residual * precond, axis=1), ("genome", "ancestry"))


def body(zscores, ld_diag, ld_next, prior_precision, chrom_cut, band_width):
    block_len = ld_diag.shape[1]
    block_count = lax.axis_size("genome")
    position = lax.axis_index("genome")
    ancestry_id = lax.axis_index("ancestry")
    following = jnp.minimum(position + 1, block_count - 1)
    inside, across = block_masks(
        block_len,
        chrom_cut[position],
        chrom_cut[following],
        band_width[position],
        band_width[following],
    )
    zero_value = jnp.zeros((), jnp.bfloat16)
    diag_tile = jnp.where(inside, ld_diag[0], zero_value)
    next_tile = jnp.where(across, ld_next[0], zero_value)
    prior_row = lax.dynamic_index_in_dim(prior_precision, ancestry_id, 0, keepdims=False)
    self_weight = lax.dynamic_index_in_dim(prior_row, ancestry_id, 0, keepdims=False)
    scaling = 1.0 / (jnp.diagonal(ld_diag[0]).astype(jnp.float32) + self_weight)
    residual = zscores[0]
    solution = jnp.zeros(residual.shape, jnp.float32)
    precond = scaling[None, :] * residual
    direction = precond
    norm_now = residual_norm(residual, precond)
    for iteration in range(ITERS):
        direction_bf = direction.astype(jnp.bfloat16)
        band_out = jnp.dot(direction_bf, diag_tile, preferred_element_type=jnp.float32)
        upper_part = passed_along(direction_bf, "genome", -1)
        band_out = band_out + lax.dot_general(
            upper_part, next_tile, (((1,), (1,)), ((), ())), preferred_element_type=jnp.float32
        )
        carried = jnp.dot(direction_bf, next_tile, preferred_element_type=jnp.float32)
        band_out = band_out + passed_along(carried.astype(jnp.bfloat16), "genome", 1).astype(
            carried.dtype
        )
        coupled = jnp.einsum(
            "b,btv->tv",
            prior_row,
            lax.all_gather(direction_bf[None], "ancestry", axis=0, tiled=True).astype(jnp.float32),
            precision=lax.Precision.HIGHEST,
        )
        image_vec = band_out + coupled
        step_len = norm_now / curvature_sum(direction, image_vec)
        solution = solution + step_len[:, None] * direction
        if iteration + 1 < ITERS:
            residual = residual - step_len[:, None] * image_vec
            precond = scaling[None, :] * residual
            norm_next = residual_norm(residual, precond)
            direction = precond + (norm_next / norm_now)[:, None] * direction
            norm_now = norm_next
    return solution[None]


def solution(mesh):
    return jax.shard_map(
        body,
        mesh=mesh,
        in_specs=(
            P("ancestry", "trait", ("groups", "genome")),
            P("ancestry", ("groups", "genome"), None),
            P("ancestry", ("groups", "genome"), None),
            P(),
            P("groups"),
            P("groups"),
        ),
        out_specs=P("ancestry", "trait", ("groups", "genome")),
        check_vma=False,
    )
```

profile of v0, /device:TPU:0, one launch (start us, length us, event | category | flops | bytes accessed | tf_op | source)
XLA Modules:
  0.0 168.3 jit_solution(2433427531543962618)
XLA Ops:
  0.0 1.4 dynamic_slice.20
  1.4 16.1 %gather_fusion = bf16[1024]{0:T(1024)(128)(2,1)S(1)} fusion(bf16[1024,1024]{1,0:T(8,128)(2,1)} %bitcast.66, s32[1024]{0:T(1024)S(1)} %bitcast.65), kind=kCustom, calls=%fused_computation | custom fusion | bytes 12288 | tf_op jit(solution)/shard_map/jit(diagonal)/cond/branch_0_fun/gather | solution.py:56
  18.3 1.3 collective-permute-start
  23.5 1.2 fusion.27
  24.7 5.6 %collective-permute-start.1 = (bf16[32,1024]{1,0:T(8,128)(2,1)S(1)}, bf16[32,1024]{1,0:T(8,128)(2,1)S(1)}, u32[]{:S(2)}, u32[]{:S(2)}) collective-permute-start(bf16[32,1024]{1,0:T(8,128)(2,1)S(1)} %fusion.27), channel_id=1, source_target_pairs={{0,4},{4,8},{8,12},{1,5},{5,9},{9,13},{2,6},{6,10},{10,14},{3,7},{... | collective-permute-start | bytes 196616 | tf_op jit(solution)/shard_map/ppermute | solution.py:12
  31.0 4.9 %all_gather.9 = bf16[2,32,1024]{2,1,0:T(8,128)(2,1)S(1)} all-gather(bf16[1,32,1024]{2,1,0:T(8,128)(2,1)S(1)} %multiply_convert_fusion.1), channel_id=1, replica_groups=mesh['groups'=2,'genome'=4,'ancestry'=2,'trait'=2] {'ancestry'}, dimensions={0}, use_global_device_ids=true | all-gather | bytes 196608 | tf_op jit(solution)/shard_map/all_gather | solution.py:76
  35.9 1.2 fusion.6
  37.5 1.9 %fusion.14 = f32[32,1024]{1,0:T(8,128)S(1)} fusion(bf16[1,1024,1024]{2,1,0:T(8,128)(2,1)S(1)} %copy-done.1, s32[]{:T(128)} %bitcast.5, pred[1024]{0:T(1024)(128)(4,1)S(1)} %fusion.48, bf16[1,32,1024]{2,1,0:T(8,128)(2,1)S(1)} %multiply_convert_fusion.1), kind=kOutput, calls=%fused_computation.18 | convolution fusion | flops 73400320 | bytes 2294788 | tf_op jit(solution)/shard_map/dot_general | solution.py:64
  39.4 3.1 %fusion.2 = bf16[1024,1024]{1,0:T(8,128)(2,1)} fusion(s32[]{:T(128)} %bitcast.5, pred[1024]{0:T(1024)(128)(4,1)S(1)} %fusion.48, bf16[1,1024,1024]{2,1,0:T(8,128)(2,1)S(1)} %copy-done.1), kind=kLoop, calls=%fused_computation.7 | loop fusion | flops 6291456 | bytes 4195332 | tf_op jit(solution)/shard_map/jit(_where)/select_n | solution.py:52
  43.1 0.9 fusion.34
  44.0 19.9 %all-reduce = (f32[32]{0:T(128)S(1)}, f32[32]{0:T(128)S(1)}) all-reduce(f32[32]{0:T(128)S(1)} %get-tuple-element.6, f32[32]{0:T(128)S(1)} %get-tuple-element.5), channel_id=1, replica_groups=mesh['groups'=2,'genome'=4,'ancestry'=2,'trait'=2] {'genome','ancestry'}, use_global_device_ids=true, to_apply=%region_1.2 | all-reduce | flops 64 | bytes 512 | tf_op jit(solution)/shard_map/psum | solution.py:35
  64.1 17.1 %psum.44 = f32[32]{0:T(128)S(1)} all-reduce(f32[32]{0:T(128)S(1)} %get-tuple-element.13), channel_id=1, replica_groups=mesh['groups'=2,'genome'=4,'ancestry'=2,'trait'=2] {'genome','ancestry'}, use_global_device_ids=true, to_apply=%region_5.6 | all-reduce | flops 32 | bytes 256 | tf_op jit(solution)/shard_map/psum | solution.py:35
  81.8 1.4 collective-permute-start.2
  83.2 5.0 %all-gather = bf16[64,1024]{1,0:T(8,128)(2,1)S(1)} all-gather(bf16[32,1024]{1,0:T(8,128)(2,1)S(1)} %get-tuple-element.11), channel_id=2, replica_groups=mesh['groups'=2,'genome'=4,'ancestry'=2,'trait'=2] {'ancestry'}, dimensions={0}, use_global_device_ids=true | all-gather | bytes 196608 | tf_op jit(solution)/shard_map/all_gather | solution.py:76
  88.2 4.5 %collective-permute-start.3 = (bf16[32,1024]{1,0:T(8,128)(2,1)S(1)}, bf16[32,1024]{1,0:T(8,128)(2,1)S(1)}, u32[]{:S(2)}, u32[]{:S(2)}) collective-permute-start(bf16[32,1024]{1,0:T(8,128)(2,1)S(1)} %convolution_convert_fusion.1), channel_id=1, source_target_pairs={{0,4},{4,8},{8,12},{1,5},{5,9},{9,13},{2,6},{6,10},{10,14},{3,7},{... | collective-permute-start | bytes 196616 | tf_op jit(solution)/shard_map/ppermute | solution.py:12
  94.7 0.8 multiply_reduce_fusion
  95.5 19.2 %psum.45 = f32[32]{0:T(128)S(1)} all-reduce(f32[32]{0:T(128)S(1)} %get-tuple-element.20), channel_id=1, replica_groups=mesh['groups'=2,'genome'=4,'ancestry'=2,'trait'=2] {'genome','ancestry'}, use_global_device_ids=true, to_apply=%region_7.8 | all-reduce | flops 32 | bytes 256 | tf_op jit(solution)/shard_map/psum | solution.py:31
  115.0 17.2 %psum.46 = f32[32]{0:T(128)S(1)} all-reduce(f32[32]{0:T(128)S(1)} %fusion.39), channel_id=1, replica_groups=mesh['groups'=2,'genome'=4,'ancestry'=2,'trait'=2] {'genome','ancestry'}, use_global_device_ids=true, to_apply=%region_9.10 | all-reduce | flops 32 | bytes 256 | tf_op jit(solution)/shard_map/psum | solution.py:35
  132.3 2.1 %fusion.58 = f32[32,1024]{1,0:T(8,128)S(1)} fusion(bf16[32,1024]{1,0:T(8,128)(2,1)S(1)} %get-tuple-element.9, bf16[1024,1024]{1,0:T(8,128)(2,1)} %fusion.2), kind=kOutput, calls=%fused_computation.84 | convolution fusion | flops 67108864 | bytes 2293760 | tf_op jit(solution)/shard_map/dot_general | solution.py:64
  134.8 1.3 collective-permute-start.4
  136.1 5.0 %all-gather.1 = bf16[64,1024]{1,0:T(8,128)(2,1)S(1)} all-gather(bf16[32,1024]{1,0:T(8,128)(2,1)S(1)} %get-tuple-element.9), channel_id=3, replica_groups=mesh['groups'=2,'genome'=4,'ancestry'=2,'trait'=2] {'ancestry'}, dimensions={0}, use_global_device_ids=true | all-gather | bytes 196608 | tf_op jit(solution)/shard_map/all_gather | solution.py:76
  141.1 4.5 %collective-permute-start.5 = (bf16[32,1024]{1,0:T(8,128)(2,1)S(1)}, bf16[32,1024]{1,0:T(8,128)(2,1)S(1)}, u32[]{:S(2)}, u32[]{:S(2)}) collective-permute-start(bf16[32,1024]{1,0:T(8,128)(2,1)S(1)} %convolution_convert_fusion), channel_id=1, source_target_pairs={{0,4},{4,8},{8,12},{1,5},{5,9},{9,13},{2,6},{6,10},{10,14},{3,7},{... | collective-permute-start | bytes 196616 | tf_op jit(solution)/shard_map/ppermute | solution.py:12
  146.2 1.3 collective-permute-done.5
  148.4 19.1 %psum.47 = f32[32]{0:T(128)S(1)} all-reduce(f32[32]{0:T(128)S(1)} %fusion.30), channel_id=1, replica_groups=mesh['groups'=2,'genome'=4,'ancestry'=2,'trait'=2] {'genome','ancestry'}, use_global_device_ids=true, to_apply=%region_11.12 | all-reduce | flops 32 | bytes 256 | tf_op jit(solution)/shard_map/psum | solution.py:31
  (47 shorter events, 10.0 us)
Async XLA Ops:
  0.0 18.2 %copy-start.2 = (f32[1,32,1024]{2,1,0:T(8,128)S(1)}, f32[1,32,1024]{2,1,0:T(8,128)}, u32[]{:S(2)}) copy-start(f32[1,32,1024]{2,1,0:T(8,128)} %param.6) | copy-start | bytes 393220
  0.0 19.6 %copy-start.6 = (s32[4]{0:T(128)S(1)}, s32[4]{0:T(128)}, u32[]{:S(2)}) copy-start(s32[4]{0:T(128)} %param.11) | copy-start | bytes 52
  0.0 19.6 %copy-start.5 = (s32[4]{0:T(128)S(1)}, s32[4]{0:T(128)}, u32[]{:S(2)}) copy-start(s32[4]{0:T(128)} %param.10) | copy-start | bytes 52
  0.0 23.5 %copy-start.3 = (bf16[1,1024,1024]{2,1,0:T(8,128)(2,1)S(1)}, bf16[1,1024,1024]{2,1,0:T(8,128)(2,1)}, u32[]{:S(2)}) copy-start(bf16[1,1024,1024]{2,1,0:T(8,128)(2,1)} %param.8) | copy-start | bytes 6291460
  18.3 24.8 %collective-permute-start = (bf16[32,1024]{1,0:T(8,128)(2,1)S(1)}, bf16[32,1024]{1,0:T(8,128)(2,1)S(1)}, u32[]{:S(2)}, u32[]{:S(2)}) collective-permute-start(bf16[32,1024]{1,0:T(8,128)(2,1)S(1)} %multiply_convert_fusion), channel_id=1, source_target_pairs={{4,0},{8,4},{12,8},{5,1},{9,5},{13,9},{6,2},{10,6},{14,10},{7,3},{... | collective-permute-start | bytes 196616 | tf_op jit(solution)/shard_map/ppermute | solution.py:12
  23.5 12.4 %copy-start.4 = (bf16[1,1024,1024]{2,1,0:T(8,128)(2,1)S(1)}, bf16[1,1024,1024]{2,1,0:T(8,128)(2,1)}, u32[]{:S(2)}) copy-start(bf16[1,1024,1024]{2,1,0:T(8,128)(2,1)} %param.8) | copy-start | bytes 6291460
  24.7 18.4 %collective-permute-start.1 = (bf16[32,1024]{1,0:T(8,128)(2,1)S(1)}, bf16[32,1024]{1,0:T(8,128)(2,1)S(1)}, u32[]{:S(2)}, u32[]{:S(2)}) collective-permute-start(bf16[32,1024]{1,0:T(8,128)(2,1)S(1)} %fusion.27), channel_id=1, source_target_pairs={{0,4},{4,8},{8,12},{1,5},{5,9},{9,13},{2,6},{6,10},{10,14},{3,7},{... | collective-permute-start | bytes 196616 | tf_op jit(solution)/shard_map/ppermute | solution.py:12
  35.9 1.6 copy-start.1
  39.4 3.1 %copy-start.7 = (f32[2,2]{1,0:T(2,128)S(1)}, f32[2,2]{1,0:T(2,128)}, u32[]{:S(2)}) copy-start(f32[2,2]{1,0:T(2,128)} %param.9) | copy-start | bytes 52
  81.2 11.6 %copy-start = (bf16[1024,1024]{1,0:T(8,128)(2,1)S(1)}, bf16[1024,1024]{1,0:T(8,128)(2,1)}, u32[]{:S(2)}) copy-start(bf16[1024,1024]{1,0:T(8,128)(2,1)} %fusion.2) | copy-start | bytes 6291460
  81.8 12.9 %collective-permute-start.2 = (bf16[32,1024]{1,0:T(8,128)(2,1)S(1)}, bf16[32,1024]{1,0:T(8,128)(2,1)S(1)}, u32[]{:S(2)}, u32[]{:S(2)}) collective-permute-start(bf16[32,1024]{1,0:T(8,128)(2,1)S(1)} %get-tuple-element.11), channel_id=1, source_target_pairs={{4,0},{8,4},{12,8},{5,1},{9,5},{13,9},{6,2},{10,6},{14,10},{7,3},{... | collective-permute-start | bytes 196616 | tf_op jit(solution)/shard_map/ppermute | solution.py:12
  88.2 6.4 %collective-permute-start.3 = (bf16[32,1024]{1,0:T(8,128)(2,1)S(1)}, bf16[32,1024]{1,0:T(8,128)(2,1)S(1)}, u32[]{:S(2)}, u32[]{:S(2)}) collective-permute-start(bf16[32,1024]{1,0:T(8,128)(2,1)S(1)} %convolution_convert_fusion.1), channel_id=1, source_target_pairs={{0,4},{4,8},{8,12},{1,5},{5,9},{9,13},{2,6},{6,10},{10,14},{3,7},{... | collective-permute-start | bytes 196616 | tf_op jit(solution)/shard_map/ppermute | solution.py:12
  134.8 12.7 %collective-permute-start.4 = (bf16[32,1024]{1,0:T(8,128)(2,1)S(1)}, bf16[32,1024]{1,0:T(8,128)(2,1)S(1)}, u32[]{:S(2)}, u32[]{:S(2)}) collective-permute-start(bf16[32,1024]{1,0:T(8,128)(2,1)S(1)} %get-tuple-element.9), channel_id=1, source_target_pairs={{4,0},{8,4},{12,8},{5,1},{9,5},{13,9},{6,2},{10,6},{14,10},{7,3},{... | collective-permute-start | bytes 196616 | tf_op jit(solution)/shard_map/ppermute | solution.py:12
  141.1 6.4 %collective-permute-start.5 = (bf16[32,1024]{1,0:T(8,128)(2,1)S(1)}, bf16[32,1024]{1,0:T(8,128)(2,1)S(1)}, u32[]{:S(2)}, u32[]{:S(2)}) collective-permute-start(bf16[32,1024]{1,0:T(8,128)(2,1)S(1)} %convolution_convert_fusion), channel_id=1, source_target_pairs={{0,4},{4,8},{8,12},{1,5},{5,9},{9,13},{2,6},{6,10},{10,14},{3,7},{... | collective-permute-start | bytes 196616 | tf_op jit(solution)/shard_map/ppermute | solution.py:12
where the time goes:
time: 169 us; the launch traced here: 168 us
  blocking collectives  108 us (64%)
  local copies, waits for them, and re-layouts  18.6 us (11%)
  starting transfers between devices  18.6 us (11%)
  matrix products  10.7 us (6%)
  other arithmetic  8.43 us (5%)
  waiting for transfers between devices  2.16 us (1%)
  between operations  2.13 us (1%)
    psum x3, blocking collectives, residual_norm(): return lax.psum(jnp.sum(residual * precond, axis=1), ('genome', 'ancestry'))  54.3 us
    psum x2, blocking collectives, curvature_sum(): lax.psum(jnp.sum(direction * image_vec, axis=1), ('genome', 'ancestry'))  38.4 us
    ppermute x6, starting transfers between devices, passed_along(): lax.ppermute(value, axis, [(source, source + steps) for source in range(l...  18.6 us
    gather x1, local copies, waits for them, and re-layouts, body(): scaling = 1.0 / (jnp.diagonal(ld_diag[0]).astype(jnp.float32) + self_weight)  16.1 us
    all_gather x3, blocking collectives, body(): lax.all_gather(direction_bf[None], 'ancestry', axis=0, tiled=True)  14.9 us
    dot_general x3, matrix products, body(): jnp.dot(direction_bf, diag_tile, preferred_element_type=jnp.float32)  4.38 us
  transfers between devices with their start and end apart: 6, of which 2 were waited for; matrix products, arithmetic and copies ran while one was open for 7% of the time, Pallas kernels for 0%

commit v1 on v0

--- a/solution.py
+++ b/solution.py
@@ -28,7 +28,7 @@
 
 
 def curvature_sum(direction, image_vec):
-    return lax.psum(jnp.sum(direction * image_vec, axis=1), ("genome", "ancestry"))
+    return lax.psum(lax.psum(jnp.sum(direction * image_vec, axis=1), "ancestry"), "genome")
 
 
 def residual_norm(residual, precond):

time: 169 us -> 178 us (1.053)
  blocking collectives: 108 us -> 116 us
    psum x2 -> x6, blocking collectives: 38.4 us -> 46.6 us  [the longest x3 31.7 us: curvature_sum(): lax.psum(lax.psum(jnp.sum(direction * image_vec, axis=1), 'ancestry'), 'g...]
where the time goes in v1:
time: 178 us; the launch traced here: 177 us
  blocking collectives  116 us (65%)
  starting transfers between devices  18.7 us (11%)
  local copies, waits for them, and re-layouts  18.6 us (10%)
  matrix products  10.7 us (6%)
  other arithmetic  8.43 us (5%)
  waiting for transfers between devices  2.16 us (1%)
  between operations  2.13 us (1%)
    psum x3, blocking collectives, residual_norm(): return lax.psum(jnp.sum(residual * precond, axis=1), ('genome', 'ancestry'))  55 us
    psum x3, blocking collectives, curvature_sum(): lax.psum(lax.psum(jnp.sum(direction * image_vec, axis=1), 'ancestry'), 'g...  31.7 us
    ppermute x6, starting transfers between devices, passed_along(): lax.ppermute(value, axis, [(source, source + steps) for source in range(l...  18.7 us
    gather x1, local copies, waits for them, and re-layouts, body(): scaling = 1.0 / (jnp.diagonal(ld_diag[0]).astype(jnp.float32) + self_weight)  16.1 us
    all_gather x3, blocking collectives, body(): lax.all_gather(direction_bf[None], 'ancestry', axis=0, tiled=True)  14.8 us
    psum x3, blocking collectives, curvature_sum(): lax.psum(jnp.sum(direction * image_vec, axis=1), 'ancestry')  14.8 us
    dot_general x3, matrix products, body(): jnp.dot(direction_bf, diag_tile, preferred_element_type=jnp.float32)  4.38 us
  transfers between devices with their start and end apart: 6, of which 2 were waited for; matrix products, arithmetic and copies ran while one was open for 7% of the time, Pallas kernels for 0%

profile of v1, /device:TPU:0, one launch (start us, length us, event | category | flops | bytes accessed | tf_op | source)
XLA Modules:
  0.0 177.1 jit_solution(5253529585163465881)
XLA Ops:
  0.0 1.4 dynamic_slice.20
  1.4 16.1 %gather_fusion = bf16[1024]{0:T(1024)(128)(2,1)S(1)} fusion(bf16[1024,1024]{1,0:T(8,128)(2,1)} %bitcast.66, s32[1024]{0:T(1024)S(1)} %bitcast.65), kind=kCustom, calls=%fused_computation | custom fusion | bytes 12288 | tf_op jit(solution)/shard_map/jit(diagonal)/cond/branch_0_fun/gather | solution.py:56
  18.3 1.3 collective-permute-start
  24.7 5.6 %collective-permute-start.1 = (bf16[32,1024]{1,0:T(8,128)(2,1)S(1)}, bf16[32,1024]{1,0:T(8,128)(2,1)S(1)}, u32[]{:S(2)}, u32[]{:S(2)}) collective-permute-start(bf16[32,1024]{1,0:T(8,128)(2,1)S(1)} %fusion.27), channel_id=1, source_target_pairs={{0,4},{4,8},{8,12},{1,5},{5,9},{9,13},{2,6},{6,10},{10,14},{3,7},{... | collective-permute-start | bytes 196616 | tf_op jit(solution)/shard_map/ppermute | solution.py:12
  31.0 4.9 %all_gather.9 = bf16[2,32,1024]{2,1,0:T(8,128)(2,1)S(1)} all-gather(bf16[1,32,1024]{2,1,0:T(8,128)(2,1)S(1)} %multiply_convert_fusion.1), channel_id=1, replica_groups=mesh['groups'=2,'genome'=4,'ancestry'=2,'trait'=2] {'ancestry'}, dimensions={0}, use_global_device_ids=true | all-gather | bytes 196608 | tf_op jit(solution)/shard_map/all_gather | solution.py:76
  37.5 1.9 %fusion.14 = f32[32,1024]{1,0:T(8,128)S(1)} fusion(bf16[1,1024,1024]{2,1,0:T(8,128)(2,1)S(1)} %copy-done.1, s32[]{:T(128)} %bitcast.5, pred[1024]{0:T(1024)(128)(4,1)S(1)} %fusion.48, bf16[1,32,1024]{2,1,0:T(8,128)(2,1)S(1)} %multiply_convert_fusion.1), kind=kOutput, calls=%fused_computation.18 | convolution fusion | flops 73400320 | bytes 2294788 | tf_op jit(solution)/shard_map/dot_general | solution.py:64
  39.4 3.1 %fusion.2 = bf16[1024,1024]{1,0:T(8,128)(2,1)} fusion(s32[]{:T(128)} %bitcast.5, pred[1024]{0:T(1024)(128)(4,1)S(1)} %fusion.48, bf16[1,1024,1024]{2,1,0:T(8,128)(2,1)S(1)} %copy-done.1), kind=kLoop, calls=%fused_computation.7 | loop fusion | flops 6291456 | bytes 4195332 | tf_op jit(solution)/shard_map/jit(_where)/select_n | solution.py:52
  44.0 4.9 %psum.64 = f32[32]{0:T(128)S(1)} all-reduce(f32[32]{0:T(128)S(1)} %get-tuple-element.5), channel_id=1, replica_groups=mesh['groups'=2,'genome'=4,'ancestry'=2,'trait'=2] {'ancestry'}, use_global_device_ids=true, to_apply=%region_3.4 | all-reduce | flops 32 | bytes 256 | tf_op jit(solution)/shard_map/psum | solution.py:31
  48.9 10.3 %psum.65 = f32[32]{0:T(128)S(1)} all-reduce(f32[32]{0:T(128)S(1)} %psum.64), channel_id=1, replica_groups=mesh['groups'=2,'genome'=4,'ancestry'=2,'trait'=2] {'genome'}, use_global_device_ids=true, to_apply=%region_4.5 | all-reduce | flops 32 | bytes 256 | tf_op jit(solution)/shard_map/psum | solution.py:31
  59.3 18.7 %psum.63 = f32[32]{0:T(128)S(1)} all-reduce(f32[32]{0:T(128)S(1)} %get-tuple-element.6), channel_id=1, replica_groups=mesh['groups'=2,'genome'=4,'ancestry'=2,'trait'=2] {'genome','ancestry'}, use_global_device_ids=true, to_apply=%region_1.2 | all-reduce | flops 32 | bytes 256 | tf_op jit(solution)/shard_map/psum | solution.py:35
  78.2 17.5 %psum.66 = f32[32]{0:T(128)S(1)} all-reduce(f32[32]{0:T(128)S(1)} %get-tuple-element.11), channel_id=1, replica_groups=mesh['groups'=2,'genome'=4,'ancestry'=2,'trait'=2] {'genome','ancestry'}, use_global_device_ids=true, to_apply=%region_6.7 | all-reduce | flops 32 | bytes 256 | tf_op jit(solution)/shard_map/psum | solution.py:35
  96.3 1.4 collective-permute-start.2
  97.7 4.9 %all-gather = bf16[64,1024]{1,0:T(8,128)(2,1)S(1)} all-gather(bf16[32,1024]{1,0:T(8,128)(2,1)S(1)} %get-tuple-element.9), channel_id=2, replica_groups=mesh['groups'=2,'genome'=4,'ancestry'=2,'trait'=2] {'ancestry'}, dimensions={0}, use_global_device_ids=true | all-gather | bytes 196608 | tf_op jit(solution)/shard_map/all_gather | solution.py:76
  102.7 4.5 %collective-permute-start.3 = (bf16[32,1024]{1,0:T(8,128)(2,1)S(1)}, bf16[32,1024]{1,0:T(8,128)(2,1)S(1)}, u32[]{:S(2)}, u32[]{:S(2)}) collective-permute-start(bf16[32,1024]{1,0:T(8,128)(2,1)S(1)} %convolution_convert_fusion.1), channel_id=1, source_target_pairs={{0,4},{4,8},{8,12},{1,5},{5,9},{9,13},{2,6},{6,10},{10,14},{3,7},{... | collective-permute-start | bytes 196616 | tf_op jit(solution)/shard_map/ppermute | solution.py:12
  109.9 4.9 %psum.67 = f32[32]{0:T(128)S(1)} all-reduce(f32[32]{0:T(128)S(1)} %get-tuple-element.18), channel_id=1, replica_groups=mesh['groups'=2,'genome'=4,'ancestry'=2,'trait'=2] {'ancestry'}, use_global_device_ids=true, to_apply=%region_8.9 | all-reduce | flops 32 | bytes 256 | tf_op jit(solution)/shard_map/psum | solution.py:31
  114.9 10.7 %psum.68 = f32[32]{0:T(128)S(1)} all-reduce(f32[32]{0:T(128)S(1)} %psum.67), channel_id=1, replica_groups=mesh['groups'=2,'genome'=4,'ancestry'=2,'trait'=2] {'genome'}, use_global_device_ids=true, to_apply=%region_9.10 | all-reduce | flops 32 | bytes 256 | tf_op jit(solution)/shard_map/psum | solution.py:31
  125.8 18.7 %psum.69 = f32[32]{0:T(128)S(1)} all-reduce(f32[32]{0:T(128)S(1)} %fusion.39), channel_id=1, replica_groups=mesh['groups'=2,'genome'=4,'ancestry'=2,'trait'=2] {'genome','ancestry'}, use_global_device_ids=true, to_apply=%region_11.12 | all-reduce | flops 32 | bytes 256 | tf_op jit(solution)/shard_map/psum | solution.py:35
  144.6 2.1 %fusion.58 = f32[32,1024]{1,0:T(8,128)S(1)} fusion(bf16[32,1024]{1,0:T(8,128)(2,1)S(1)} %get-tuple-element.7, bf16[1024,1024]{1,0:T(8,128)(2,1)} %fusion.2), kind=kOutput, calls=%fused_computation.84 | convolution fusion | flops 67108864 | bytes 2293760 | tf_op jit(solution)/shard_map/dot_general | solution.py:64
  147.2 1.3 collective-permute-start.4
  148.5 4.9 %all-gather.1 = bf16[64,1024]{1,0:T(8,128)(2,1)S(1)} all-gather(bf16[32,1024]{1,0:T(8,128)(2,1)S(1)} %get-tuple-element.7), channel_id=3, replica_groups=mesh['groups'=2,'genome'=4,'ancestry'=2,'trait'=2] {'ancestry'}, dimensions={0}, use_global_device_ids=true | all-gather | bytes 196608 | tf_op jit(solution)/shard_map/all_gather | solution.py:76
  153.4 4.5 %collective-permute-start.5 = (bf16[32,1024]{1,0:T(8,128)(2,1)S(1)}, bf16[32,1024]{1,0:T(8,128)(2,1)S(1)}, u32[]{:S(2)}, u32[]{:S(2)}) collective-permute-start(bf16[32,1024]{1,0:T(8,128)(2,1)S(1)} %convolution_convert_fusion), channel_id=1, source_target_pairs={{0,4},{4,8},{8,12},{1,5},{5,9},{9,13},{2,6},{6,10},{10,14},{3,7},{... | collective-permute-start | bytes 196616 | tf_op jit(solution)/shard_map/ppermute | solution.py:12
  158.5 1.3 collective-permute-done.5
  160.7 4.9 %psum.70 = f32[32]{0:T(128)S(1)} all-reduce(f32[32]{0:T(128)S(1)} %fusion.30), channel_id=1, replica_groups=mesh['groups'=2,'genome'=4,'ancestry'=2,'trait'=2] {'ancestry'}, use_global_device_ids=true, to_apply=%region_13.14 | all-reduce | flops 32 | bytes 256 | tf_op jit(solution)/shard_map/psum | solution.py:31
  165.6 10.7 %psum.71 = f32[32]{0:T(128)S(1)} all-reduce(f32[32]{0:T(128)S(1)} %psum.70), channel_id=1, replica_groups=mesh['groups'=2,'genome'=4,'ancestry'=2,'trait'=2] {'genome'}, use_global_device_ids=true, to_apply=%region_14.15 | all-reduce | flops 32 | bytes 256 | tf_op jit(solution)/shard_map/psum | solution.py:31
  (51 shorter events, 14.0 us)
Async XLA Ops:
  0.0 18.2 %copy-start.2 = (f32[1,32,1024]{2,1,0:T(8,128)S(1)}, f32[1,32,1024]{2,1,0:T(8,128)}, u32[]{:S(2)}) copy-start(f32[1,32,1024]{2,1,0:T(8,128)} %param.6) | copy-start | bytes 393220
  0.0 19.6 %copy-start.6 = (s32[4]{0:T(128)S(1)}, s32[4]{0:T(128)}, u32[]{:S(2)}) copy-start(s32[4]{0:T(128)} %param.11) | copy-start | bytes 52
  0.0 19.6 %copy-start.5 = (s32[4]{0:T(128)S(1)}, s32[4]{0:T(128)}, u32[]{:S(2)}) copy-start(s32[4]{0:T(128)} %param.10) | copy-start | bytes 52
  0.0 23.5 %copy-start.3 = (bf16[1,1024,1024]{2,1,0:T(8,128)(2,1)S(1)}, bf16[1,1024,1024]{2,1,0:T(8,128)(2,1)}, u32[]{:S(2)}) copy-start(bf16[1,1024,1024]{2,1,0:T(8,128)(2,1)} %param.8) | copy-start | bytes 6291460
  18.3 24.8 %collective-permute-start = (bf16[32,1024]{1,0:T(8,128)(2,1)S(1)}, bf16[32,1024]{1,0:T(8,128)(2,1)S(1)}, u32[]{:S(2)}, u32[]{:S(2)}) collective-permute-start(bf16[32,1024]{1,0:T(8,128)(2,1)S(1)} %multiply_convert_fusion), channel_id=1, source_target_pairs={{4,0},{8,4},{12,8},{5,1},{9,5},{13,9},{6,2},{10,6},{14,10},{7,3},{... | collective-permute-start | bytes 196616 | tf_op jit(solution)/shard_map/ppermute | solution.py:12
  23.5 12.4 %copy-start.4 = (bf16[1,1024,1024]{2,1,0:T(8,128)(2,1)S(1)}, bf16[1,1024,1024]{2,1,0:T(8,128)(2,1)}, u32[]{:S(2)}) copy-start(bf16[1,1024,1024]{2,1,0:T(8,128)(2,1)} %param.8) | copy-start | bytes 6291460
  24.7 18.4 %collective-permute-start.1 = (bf16[32,1024]{1,0:T(8,128)(2,1)S(1)}, bf16[32,1024]{1,0:T(8,128)(2,1)S(1)}, u32[]{:S(2)}, u32[]{:S(2)}) collective-permute-start(bf16[32,1024]{1,0:T(8,128)(2,1)S(1)} %fusion.27), channel_id=1, source_target_pairs={{0,4},{4,8},{8,12},{1,5},{5,9},{9,13},{2,6},{6,10},{10,14},{3,7},{... | collective-permute-start | bytes 196616 | tf_op jit(solution)/shard_map/ppermute | solution.py:12
  35.9 1.6 copy-start.1
  39.4 3.1 %copy-start.7 = (f32[2,2]{1,0:T(2,128)S(1)}, f32[2,2]{1,0:T(2,128)}, u32[]{:S(2)}) copy-start(f32[2,2]{1,0:T(2,128)} %param.9) | copy-start | bytes 52
  95.7 11.5 %copy-start = (bf16[1024,1024]{1,0:T(8,128)(2,1)S(1)}, bf16[1024,1024]{1,0:T(8,128)(2,1)}, u32[]{:S(2)}) copy-start(bf16[1024,1024]{1,0:T(8,128)(2,1)} %fusion.2) | copy-start | bytes 6291460
  96.3 12.8 %collective-permute-start.2 = (bf16[32,1024]{1,0:T(8,128)(2,1)S(1)}, bf16[32,1024]{1,0:T(8,128)(2,1)S(1)}, u32[]{:S(2)}, u32[]{:S(2)}) collective-permute-start(bf16[32,1024]{1,0:T(8,128)(2,1)S(1)} %get-tuple-element.9), channel_id=1, source_target_pairs={{4,0},{8,4},{12,8},{5,1},{9,5},{13,9},{6,2},{10,6},{14,10},{7,3},{... | collective-permute-start | bytes 196616 | tf_op jit(solution)/shard_map/ppermute | solution.py:12
  102.7 6.4 %collective-permute-start.3 = (bf16[32,1024]{1,0:T(8,128)(2,1)S(1)}, bf16[32,1024]{1,0:T(8,128)(2,1)S(1)}, u32[]{:S(2)}, u32[]{:S(2)}) collective-permute-start(bf16[32,1024]{1,0:T(8,128)(2,1)S(1)} %convolution_convert_fusion.1), channel_id=1, source_target_pairs={{0,4},{4,8},{8,12},{1,5},{5,9},{9,13},{2,6},{6,10},{10,14},{3,7},{... | collective-permute-start | bytes 196616 | tf_op jit(solution)/shard_map/ppermute | solution.py:12
  147.2 12.7 %collective-permute-start.4 = (bf16[32,1024]{1,0:T(8,128)(2,1)S(1)}, bf16[32,1024]{1,0:T(8,128)(2,1)S(1)}, u32[]{:S(2)}, u32[]{:S(2)}) collective-permute-start(bf16[32,1024]{1,0:T(8,128)(2,1)S(1)} %get-tuple-element.7), channel_id=1, source_target_pairs={{4,0},{8,4},{12,8},{5,1},{9,5},{13,9},{6,2},{10,6},{14,10},{7,3},{... | collective-permute-start | bytes 196616 | tf_op jit(solution)/shard_map/ppermute | solution.py:12
  153.4 6.4 %collective-permute-start.5 = (bf16[32,1024]{1,0:T(8,128)(2,1)S(1)}, bf16[32,1024]{1,0:T(8,128)(2,1)S(1)}, u32[]{:S(2)}, u32[]{:S(2)}) collective-permute-start(bf16[32,1024]{1,0:T(8,128)(2,1)S(1)} %convolution_convert_fusion), channel_id=1, source_target_pairs={{0,4},{4,8},{8,12},{1,5},{5,9},{9,13},{2,6},{6,10},{10,14},{3,7},{... | collective-permute-start | bytes 196616 | tf_op jit(solution)/shard_map/ppermute | solution.py:12
